TPU v7x, 32 devices: a whole 2x2x4 slice. The times are simulated.
32 devices in a mesh: groups: 2 (over y), tiles: 16 (over z, x, core).
Axes of the slice: x: 2, y: 2, z: 4, core: 2. Of those that a mesh axis runs over, the one named last changes fastest.
Arguments:
- raw: bfloat16 [16, 256, 2048], P(None, ('groups', 'tiles')), parts along dimension 1, may hold values from -40 to 40, as said below
- fir: float32 [64], replicated, may hold values from -0.75 to 0.75
- keep: int32 [16, 256], P(None, ('groups', 'tiles')), parts along dimension 1, may hold values 0 or 1
- table: int32 [16, 2], replicated, may hold values from 0 to 0, as said below
Outputs:
- stacks: bfloat16 [32, 128, 128, 256], P(('groups', 'tiles')), parts along dimension 0
There are 2 independent parts, one for each index of `groups`. A program takes and returns all parts, laid end to end along the dimension named above; an argument that names none is the same for every part. Nothing has to cross between parts.
Inputs may be any that keep to these rules, and one draw needn't show every extreme that they name: `table`: each row holds r <= c. `raw`: a common motion of all channels plus independent noise.
All inputs are finite; a program needn't handle non-finite values. No bound on the sum of `keep` on one device may be relied on, other than what follows from the above.
Results may differ from a plain program's by a relative error of at most 0.0053.
Values may be sent and summed in bfloat16 or wider, within the bound.
A program may use at most 128 MiB of HBM per device.

v0:
```python
import jax
import jax.numpy as jnp
from jax import lax
from jax.sharding import PartitionSpec as P

WINDOWS = 16
TILE = 128
SEG = 512
LAGS = 256
TAPS = 64
DEC = 4
RAW = 2048
NBIN = 256


def filter_band(fir):
    period = 2 * RAW + TAPS
    pattern = jnp.concatenate([fir[:1], jnp.zeros((period - TAPS,), jnp.float32), fir[1:][::-1]])
    tiled = jnp.tile(pattern, SEG)[: SEG * (period - DEC)].reshape(SEG, period - DEC)
    return tiled[:, :RAW]


def filter_block(raw, fir):
    band = filter_band(fir)
    return jnp.einsum("wcm,nm->wcn", raw.astype(jnp.float32), band, precision=lax.Precision.HIGHEST)


def dft_tables():
    steps = jnp.arange(SEG, dtype=jnp.int32)
    freqs = jnp.arange(NBIN, dtype=jnp.int32)
    angle = 2.0 * jnp.pi / SEG * jnp.mod(steps[:, None] * freqs[None, :], SEG).astype(jnp.float32)
    return (jnp.cos(angle), jnp.sin(angle))


def whiten(decimated, keep):
    cosine, sine = dft_tables()
    real_part = jnp.einsum("wcn,nf->wcf", decimated, cosine, precision=lax.Precision.HIGHEST)
    imag_part = -jnp.einsum("wcn,nf->wcf", decimated, sine, precision=lax.Precision.HIGHEST)
    power = real_part * real_part + imag_part * imag_part
    level = jnp.mean(power, -1, keepdims=True)
    scale = keep.astype(jnp.float32)[..., None] / jnp.sqrt(0.5 * power + 0.5 * level + 1e-05)
    return jnp.concatenate([real_part * scale, imag_part * scale], -1).astype(jnp.bfloat16)


def cross_tile(rows, cols):
    half = rows.shape[-1] // 2
    row_re, row_im = (rows[..., :half], rows[..., half:])
    col_re, col_im = (cols[..., :half], cols[..., half:])
    cross_re = jnp.einsum("wif,wjf->ijf", row_re, col_re, preferred_element_type=jnp.float32)
    cross_re = cross_re + jnp.einsum(
        "wif,wjf->ijf", row_im, col_im, preferred_element_type=jnp.float32
    )
    cross_im = jnp.einsum("wif,wjf->ijf", row_re, col_im, preferred_element_type=jnp.float32)
    cross_im = cross_im - jnp.einsum(
        "wif,wjf->ijf", row_im, col_re, preferred_element_type=jnp.float32
    )
    return jnp.concatenate([cross_re, cross_im], -1).astype(jnp.bfloat16)


def lag_rows(freqs, imaginary):
    shifts = jnp.arange(LAGS, dtype=jnp.int32) - LAGS // 2
    angle = 2.0 * jnp.pi / SEG * jnp.mod(freqs[:, None] * shifts[None, :], SEG).astype(jnp.float32)
    weight = jnp.where(freqs == 0, 1.0, 2.0).astype(jnp.float32)[:, None] / jnp.sqrt(
        jnp.float32(WINDOWS * NBIN)
    )
    return jnp.where(imaginary[:, None], -weight * jnp.sin(angle), weight * jnp.cos(angle)).astype(
        jnp.bfloat16
    )


def local(raw, fir, keep, table):
    devices = lax.axis_size("tiles")
    filtered = filter_block(raw, fir)
    channel_sum = lax.psum(jnp.sum(filtered, 1), "tiles")
    common = channel_sum[:, None, :] / (raw.shape[1] * devices)
    whitened = whiten(filtered - common, keep)
    entry = table[lax.axis_index("tiles")]
    row_base = entry[0] * TILE
    col_base = entry[1] * TILE
    offsets = jnp.arange(TILE, dtype=jnp.int32)
    piece = lax.all_gather(whitened, "tiles", axis=1, tiled=True)
    places = jnp.arange(piece.shape[1], dtype=jnp.int32)
    pick_rows = (places[None, :] == row_base + offsets[:, None]).astype(jnp.bfloat16)
    pick_cols = (places[None, :] == col_base + offsets[:, None]).astype(jnp.bfloat16)
    add_rows = jnp.einsum("in,wnf->wif", pick_rows, piece, preferred_element_type=jnp.float32)
    add_cols = jnp.einsum("in,wnf->wif", pick_cols, piece, preferred_element_type=jnp.float32)
    rows = add_rows.astype(jnp.bfloat16)
    cols = add_cols.astype(jnp.bfloat16)
    cross = cross_tile(rows, cols).reshape(TILE * TILE, 2 * NBIN)
    freqs = jnp.concatenate([jnp.arange(NBIN, dtype=jnp.int32)] * 2)
    imaginary = jnp.arange(2 * NBIN, dtype=jnp.int32) >= NBIN
    lags = lag_rows(freqs, imaginary)
    stacked = jnp.dot(cross, lags, preferred_element_type=jnp.float32).astype(jnp.bfloat16)
    return stacked.reshape(1, TILE, TILE, LAGS)


def solution(mesh):
    placed = (P(None, ("groups", "tiles"), None), P(), P(None, ("groups", "tiles")), P())
    return jax.shard_map(
        local,
        mesh=mesh,
        in_specs=placed,
        out_specs=P(("groups", "tiles"), None, None, None),
        check_vma=False,
    )
```

profile of v0, /device:TPU:0, one launch (start us, length us, event | category | flops | bytes accessed | tf_op | source)
XLA Modules:
  0.0 251.8 jit_solution(16928799047254272326)
XLA Ops:
  6.5 0.8 slice.33
  7.4 0.7 concatenate.26
  8.2 3.9 %tile.4 = f32[512,4160]{1,0:T(8,128)} broadcast(f32[4160]{0:T(1024)S(1)} %concatenate.26), dimensions={1} | broadcast | bytes 8536320 | tf_op jit(solution)/shard_map/tile | solution.py:19
  12.0 10.0 %tile.10 = f32[2129920]{0:T(1024)} reshape(f32[512,4160]{1,0:T(8,128)} %tile.4) | data formatting | bytes 17039360 | tf_op jit(solution)/shard_map/tile | solution.py:19
  22.0 7.8 %slice.42 = f32[2127872]{0:T(1024)} slice(f32[2129920]{0:T(1024)} %tile.10), slice={[0:2127872]} | slice | bytes 17022976 | tf_op jit(solution)/shard_map/slice | solution.py:19
  29.8 14.4 %reshape.66 = f32[512,4156]{1,0:T(8,128)} reshape(f32[2127872]{0:T(1024)} %slice.42) | data formatting | bytes 17022976 | tf_op jit(solution)/shard_map/reshape | solution.py:19
  44.2 4.8 %fusion.70 = (f32[16,512]{1,0:T(8,128)S(1)}, f32[16,8,512]{2,0,1:T(8,128)S(1)}) fusion(bf16[16,8,2048]{2,1,0:T(8,128)(2,1)S(1)} %copy-done, f32[512,4156]{1,0:T(8,128)} %reshape.66), kind=kOutput, calls=%fused_computation.98 | convolution fusion | flops 1610670080 | bytes 5013504 | tf_op jit(solution)/shard_map/wcm,nm->wcn/dot_general | solution.py:25
  49.0 62.9 %psum.7 = f32[16,512]{1,0:T(8,128)S(1)} all-reduce(f32[16,512]{1,0:T(8,128)S(1)} %get-tuple-element.15), channel_id=1, replica_groups=mesh['groups'=2,'tiles'=16] {'tiles'}, use_global_device_ids=true, to_apply=%region_1.0 | all-reduce | flops 8192 | bytes 65536 | tf_op jit(solution)/shard_map/psum | solution.py:74
  112.0 2.4 fusion.25
  114.4 2.5 fusion.46
  117.0 0.1 multiply_convert_fusion.1
  117.1 0.7 pad_maximum_fusion
  117.9 0.6 fusion.69
  119.8 36.6 %all-gather.2.cloned.1.call-done = bf16[16,128,512]{2,1,0:T(8,128)(2,1)} async-done(((bf16[16,8,512]{2,1,0:T(8,128)(2,1)}), bf16[16,128,512]{2,1,0:T(8,128)(2,1)}) %all-gather.2.cloned.1.call-update) | async-done | bytes 2097168 | tf_op jit(solution)/shard_map/all_gather | solution.py:81
  156.4 2.4 convert_bitcast_fusion
  158.8 2.4 convert_bitcast_fusion.1
  161.2 0.3 fusion.67
  161.5 8.1 %fusion.13 = f32[256,128,128]{2,1,0:T(8,128)} fusion(bf16[16,128,256]{1,2,0:T(8,128)(2,1)S(1)} %get-tuple-element.19, bf16[16,128,256]{1,2,0:T(8,128)(2,1)S(1)} %get-tuple-element.5), kind=kOutput, calls=%fused_computation.22 | convolution fusion | flops 134217728 | bytes 18874368 | tf_op jit(solution)/shard_map/wif,wjf->ijf/dot_general | solution.py:49
  169.6 8.1 %fusion.9 = f32[256,128,128]{2,1,0:T(8,128)} fusion(bf16[16,128,256]{1,2,0:T(8,128)(2,1)S(1)} %get-tuple-element.6, bf16[16,128,256]{1,2,0:T(8,128)(2,1)S(1)} %get-tuple-element.19), kind=kOutput, calls=%fused_computation.18 | convolution fusion | flops 134217728 | bytes 18874368 | tf_op jit(solution)/shard_map/wif,wjf->ijf/dot_general | solution.py:53
  177.6 12.9 %fusion.3 = bf16[128,128,256]{0,1,2:T(8,128)(2,1)} fusion(f32[256,128,128]{2,1,0:T(8,128)} %fusion.13, bf16[16,128,256]{1,2,0:T(8,128)(2,1)S(1)} %get-tuple-element.20, bf16[16,128,256]{1,2,0:T(8,128)(2,1)S(1)} %get-tuple-element.6), kind=kOutput, calls=%fused_computation.6 | convolution fusion | flops 142606336 | bytes 27262976 | tf_op jit(solution)/shard_map/wif,wjf->ijf/dot_general | solution.py:50
  190.5 13.5 %copy.25 = bf16[128,128,256]{2,1,0:T(8,128)(2,1)} copy(bf16[128,128,256]{0,1,2:T(8,128)(2,1)} %fusion.3) | data formatting | bytes 16777216 | tf_op jit(solution)/shard_map/add | solution.py:50
  204.0 12.9 %fusion.4 = bf16[128,128,256]{0,1,2:T(8,128)(2,1)} fusion(f32[256,128,128]{2,1,0:T(8,128)} %fusion.9, bf16[16,128,256]{1,2,0:T(8,128)(2,1)S(1)} %get-tuple-element.20, bf16[16,128,256]{1,2,0:T(8,128)(2,1)S(1)} %get-tuple-element.5), kind=kOutput, calls=%fused_computation.7 | convolution fusion | flops 142606336 | bytes 27262976 | tf_op jit(solution)/shard_map/wif,wjf->ijf/dot_general | solution.py:54
  216.9 13.5 %copy.30 = bf16[128,128,256]{2,1,0:T(8,128)(2,1)} copy(bf16[128,128,256]{0,1,2:T(8,128)(2,1)} %fusion.4) | data formatting | bytes 16777216 | tf_op jit(solution)/shard_map/sub | solution.py:54
  230.4 14.5 %convolution_convert_fusion = bf16[16384,256]{1,0:T(8,128)(2,1)} fusion(bf16[16384,256]{1,0:T(8,128)(2,1)} %bitcast.40, bf16[16384,256]{1,0:T(8,128)(2,1)} %bitcast.39, f32[512]{0:T(512)S(1)} %get-tuple-element.12, s32[256]{0:T(256)S(1)} %iota_add_fusion, s32[512]{0:T(512)S(1)} %pad_add_fusion, f32[512]{0:T(512)S(1)} %get-tuple-element.11, ...), kind=kOutput, calls=%fused_computation | convolution fusion | flops 4335075328 | bytes 25173504 | tf_op jit(solution)/shard_map/dot_general | solution.py:93
  (25 shorter events, 0.4 us)
Async XLA Ops:
  6.5 37.6 %copy-start = (bf16[16,8,2048]{2,1,0:T(8,128)(2,1)S(1)}, bf16[16,8,2048]{2,1,0:T(8,128)(2,1)}, u32[]{:S(2)}) copy-start(bf16[16,8,2048]{2,1,0:T(8,128)(2,1)} %param.4) | copy-start | bytes 1572868
  6.5 149.9 %all-gather.2.cloned.1.call-start = ((), (), s32[]{:S(2)}) async-start(), calls=%async_computation | async-start | bytes 2228224 | tf_op jit(solution)/shard_map/all_gather | solution.py:81
  44.2 72.7 %copy-start.2 = (s32[16,8]{0,1:T(8,128)S(1)}, s32[16,8]{0,1:T(8,128)}, u32[]{:S(2)}) copy-start(s32[16,8]{0,1:T(8,128)} %param.6) | copy-start | bytes 1540
  44.2 73.6 %copy-start.3 = (s32[16,2]{0,1:T(2,128)S(1)}, s32[16,2]{0,1:T(2,128)}, u32[]{:S(2)}) copy-start(s32[16,2]{0,1:T(2,128)} %param.7) | copy-start | bytes 388
  230.4 14.5 %copy-start.1 = (bf16[16,8,2048]{2,1,0:T(8,128)(2,1)S(1)}, bf16[16,8,2048]{2,1,0:T(8,128)(2,1)}, u32[]{:S(2)}) copy-start(bf16[16,8,2048]{2,1,0:T(8,128)(2,1)} %param.4) | copy-start | bytes 1572868
Sparse Core Ops, SparseCore 0:
  117.9 38.4 all-gather.1
where the time goes:
time: 253 us; the launch traced here: 252 us
  matrix products  71 us (28%)
  local copies, waits for them, and re-layouts  65.6 us (26%)
  blocking collectives  62.9 us (25%)
  waiting for transfers between devices  36.6 us (14%)
  between operations  14.8 us (6%)
    psum x1, blocking collectives, local(): channel_sum = lax.psum(jnp.sum(filtered, 1), 'tiles')  62.9 us
    all_gather x1, waiting for transfers between devices, local(): piece = lax.all_gather(whitened, 'tiles', axis=1, tiled=True)  36.6 us
    dot_general x1, matrix products, local(): jnp.dot(cross, lags, preferred_element_type=jnp.float32)  14.5 us
    reshape x1, local copies, waits for them, and re-layouts, filter_band(): jnp.tile(pattern, SEG)[:SEG * (period - DEC)].reshape(SEG, period - DEC)  14.4 us
    another operation x2, local copies, waits for them, and re-layouts, filter_band(): jnp.tile(pattern, SEG)[:SEG * (period - DEC)].reshape(SEG, period - DEC)  13.8 us
    sub x1, local copies, waits for them, and re-layouts, cross_tile(): cross_im - jnp.einsum('wif,wjf->ijf', row_im, col_re, preferred_element_t...  13.5 us
    add x1, local copies, waits for them, and re-layouts, cross_tile(): cross_re + jnp.einsum('wif,wjf->ijf', row_im, col_im, preferred_element_t...  13.5 us
    dot_general x1, matrix products, cross_tile(): jnp.einsum('wif,wjf->ijf', row_im, col_re, preferred_element_type=jnp.flo...  12.9 us
  transfers between devices with their start and end apart: 1, of which 1 were waited for; matrix products, arithmetic and copies ran while one was open for 0% of the time, Pallas kernels for 0%

commit v1 on v0

--- a/solution.py
+++ b/solution.py
@@ -71,7 +71,9 @@
 def local(raw, fir, keep, table):
     devices = lax.axis_size("tiles")
     filtered = filter_block(raw, fir)
-    channel_sum = lax.psum(jnp.sum(filtered, 1), "tiles")
+    own = jnp.sum(filtered, 1)
+    shards = lax.all_gather(own, "tiles", axis=0, tiled=False)
+    channel_sum = shards.sum(axis=0)
     common = channel_sum[:, None, :] / (raw.shape[1] * devices)
     whitened = whiten(filtered - common, keep)
     entry = table[lax.axis_index("tiles")]

time: 253 us -> 215 us (0.85)
  blocking collectives: 62.9 us -> 24.8 us
    psum x1 -> x0, blocking collectives: 62.9 us -> none  [local(): channel_sum = lax.psum(jnp.sum(filtered, 1), 'tiles')]
    all_gather x0 -> x1, blocking collectives: none -> 24.8 us  [local(): shards = lax.all_gather(own, 'tiles', axis=0, tiled=False)]
where the time goes in v1:
time: 215 us; the launch traced here: 214 us
  matrix products  71.2 us (33%)
  local copies, waits for them, and re-layouts  65.6 us (31%)
  waiting for transfers between devices  36.6 us (17%)
  blocking collectives  24.8 us (12%)
  between operations  14.9 us (7%)
    all_gather x1, waiting for transfers between devices, local(): piece = lax.all_gather(whitened, 'tiles', axis=1, tiled=True)  36.6 us
    all_gather x1, blocking collectives, local(): shards = lax.all_gather(own, 'tiles', axis=0, tiled=False)  24.8 us
    dot_general x1, matrix products, local(): jnp.dot(cross, lags, preferred_element_type=jnp.float32)  14.5 us
    reshape x1, local copies, waits for them, and re-layouts, filter_band(): jnp.tile(pattern, SEG)[:SEG * (period - DEC)].reshape(SEG, period - DEC)  14.4 us
    another operation x2, local copies, waits for them, and re-layouts, filter_band(): jnp.tile(pattern, SEG)[:SEG * (period - DEC)].reshape(SEG, period - DEC)  13.8 us
    sub x1, local copies, waits for them, and re-layouts, cross_tile(): cross_im - jnp.einsum('wif,wjf->ijf', row_im, col_re, preferred_element_t...  13.5 us
    add x1, local copies, waits for them, and re-layouts, cross_tile(): cross_re + jnp.einsum('wif,wjf->ijf', row_im, col_im, preferred_element_t...  13.5 us
    dot_general x1, matrix products, cross_tile(): jnp.einsum('wif,wjf->ijf', row_im, col_re, preferred_element_type=jnp.flo...  12.9 us
  transfers between devices with their start and end apart: 1, of which 1 were waited for; matrix products, arithmetic and copies ran while one was open for 0% of the time, Pallas kernels for 0%

profile of v1, /device:TPU:0, one launch (start us, length us, event | category | flops | bytes accessed | tf_op | source)
XLA Modules:
  0.0 214.0 jit_solution(4773648077511945587)
XLA Ops:
  6.5 0.8 slice.33
  7.4 0.7 concatenate.26
  8.2 3.9 %tile.4 = f32[512,4160]{1,0:T(8,128)} broadcast(f32[4160]{0:T(1024)S(1)} %concatenate.26), dimensions={1} | broadcast | bytes 8536320 | tf_op jit(solution)/shard_map/tile | solution.py:19
  12.0 10.0 %tile.10 = f32[2129920]{0:T(1024)} reshape(f32[512,4160]{1,0:T(8,128)} %tile.4) | data formatting | bytes 17039360 | tf_op jit(solution)/shard_map/tile | solution.py:19
  22.0 7.8 %slice.42 = f32[2127872]{0:T(1024)} slice(f32[2129920]{0:T(1024)} %tile.10), slice={[0:2127872]} | slice | bytes 17022976 | tf_op jit(solution)/shard_map/slice | solution.py:19
  29.8 14.4 %reshape.68 = f32[512,4156]{1,0:T(8,128)} reshape(f32[2127872]{0:T(1024)} %slice.42) | data formatting | bytes 17022976 | tf_op jit(solution)/shard_map/reshape | solution.py:19
  44.2 4.8 %fusion.70 = (f32[16,512]{1,0:T(8,128)S(1)}, f32[16,8,512]{2,0,1:T(8,128)S(1)}) fusion(bf16[16,8,2048]{2,1,0:T(8,128)(2,1)S(1)} %copy-done, f32[512,4156]{1,0:T(8,128)} %reshape.68), kind=kOutput, calls=%fused_computation.98 | convolution fusion | flops 1610670080 | bytes 5013504 | tf_op jit(solution)/shard_map/wcm,nm->wcn/dot_general | solution.py:25
  49.0 24.8 %all-gather = f32[256,512]{1,0:T(8,128)S(1)} all-gather(f32[16,512]{1,0:T(8,128)S(1)} %get-tuple-element.15), channel_id=2, replica_groups=mesh['groups'=2,'tiles'=16] {'tiles'}, dimensions={0}, use_global_device_ids=true | all-gather | bytes 557056 | tf_op jit(solution)/shard_map/all_gather | solution.py:75
  73.9 2.4 %fusion.25 = f32[16,8,256]{2,1,0:T(8,128)S(1)} fusion(f32[16,8,512]{2,0,1:T(8,128)S(1)} %broadcast_subtract_fusion), kind=kOutput, calls=%fused_computation.39 | convolution fusion | flops 203161600 | bytes 393216 | tf_op jit(solution)/shard_map/wcn,nf->wcf/dot_general | solution.py:37
  76.3 2.5 %fusion.46 = (f32[16,8]{1,0:T(8,128)S(1)}, f32[16,8,256]{2,1,0:T(8,128)S(1)}) fusion(f32[16,8,256]{2,1,0:T(8,128)S(1)} %fusion.25, f32[16,8,512]{2,0,1:T(8,128)S(1)} %broadcast_subtract_fusion), kind=kOutput, calls=%fused_computation.65 | convolution fusion | flops 203292544 | bytes 524800 | tf_op jit(solution)/shard_map/wcn,nf->wcf/dot_general | solution.py:38
  78.9 0.1 multiply_convert_fusion.1
  79.0 0.7 pad_maximum_fusion
  79.7 0.6 fusion.69
  81.7 36.6 %all-gather.3.cloned.1.call-done = bf16[16,128,512]{2,1,0:T(8,128)(2,1)} async-done(((bf16[16,8,512]{2,1,0:T(8,128)(2,1)}), bf16[16,128,512]{2,1,0:T(8,128)(2,1)}) %all-gather.3.cloned.1.call-update) | async-done | bytes 2097168 | tf_op jit(solution)/shard_map/all_gather | solution.py:83
  118.3 2.4 %convert_bitcast_fusion = bf16[16,128,512]{1,2,0:T(8,128)(2,1)S(1)} fusion(bf16[16,128,512]{2,1,0:T(8,128)(2,1)} %all-gather.3.cloned.1.call-done, s32[128]{0:T(128)S(1)} %iota_add_fusion.1), kind=kOutput, calls=%fused_computation.10 | convolution fusion | flops 269500416 | bytes 4194816 | tf_op jit(solution)/shard_map/in,wnf->wif/dot_general | solution.py:87
  120.7 2.4 %convert_bitcast_fusion.1 = bf16[16,128,512]{1,2,0:T(8,128)(2,1)S(1)} fusion(bf16[16,128,512]{2,1,0:T(8,128)(2,1)} %all-gather.3.cloned.1.call-done, s32[128]{0:T(128)S(1)} %iota_add_fusion.2), kind=kOutput, calls=%fused_computation.11 | convolution fusion | flops 269500416 | bytes 4194816 | tf_op jit(solution)/shard_map/in,wnf->wif/dot_general | solution.py:88
  123.1 0.3 fusion.67
  123.4 8.3 %fusion.13 = f32[256,128,128]{2,1,0:T(8,128)} fusion(bf16[16,128,256]{1,2,0:T(8,128)(2,1)S(1)} %get-tuple-element.19, bf16[16,128,256]{1,2,0:T(8,128)(2,1)S(1)} %get-tuple-element.5), kind=kOutput, calls=%fused_computation.22 | convolution fusion | flops 134217728 | bytes 18874368 | tf_op jit(solution)/shard_map/wif,wjf->ijf/dot_general | solution.py:49
  131.7 8.1 %fusion.9 = f32[256,128,128]{2,1,0:T(8,128)} fusion(bf16[16,128,256]{1,2,0:T(8,128)(2,1)S(1)} %get-tuple-element.6, bf16[16,128,256]{1,2,0:T(8,128)(2,1)S(1)} %get-tuple-element.19), kind=kOutput, calls=%fused_computation.18 | convolution fusion | flops 134217728 | bytes 18874368 | tf_op jit(solution)/shard_map/wif,wjf->ijf/dot_general | solution.py:53
  139.8 12.9 %fusion.3 = bf16[128,128,256]{0,1,2:T(8,128)(2,1)} fusion(f32[256,128,128]{2,1,0:T(8,128)} %fusion.13, bf16[16,128,256]{1,2,0:T(8,128)(2,1)S(1)} %get-tuple-element.20, bf16[16,128,256]{1,2,0:T(8,128)(2,1)S(1)} %get-tuple-element.6), kind=kOutput, calls=%fused_computation.6 | convolution fusion | flops 142606336 | bytes 27262976 | tf_op jit(solution)/shard_map/wif,wjf->ijf/dot_general | solution.py:50
  152.7 13.5 %copy.39 = bf16[128,128,256]{2,1,0:T(8,128)(2,1)} copy(bf16[128,128,256]{0,1,2:T(8,128)(2,1)} %fusion.3) | data formatting | bytes 16777216 | tf_op jit(solution)/shard_map/add | solution.py:50
  166.1 12.9 %fusion.4 = bf16[128,128,256]{0,1,2:T(8,128)(2,1)} fusion(f32[256,128,128]{2,1,0:T(8,128)} %fusion.9, bf16[16,128,256]{1,2,0:T(8,128)(2,1)S(1)} %get-tuple-element.20, bf16[16,128,256]{1,2,0:T(8,128)(2,1)S(1)} %get-tuple-element.5), kind=kOutput, calls=%fused_computation.7 | convolution fusion | flops 142606336 | bytes 27262976 | tf_op jit(solution)/shard_map/wif,wjf->ijf/dot_general | solution.py:54
  179.1 13.5 %copy.44 = bf16[128,128,256]{2,1,0:T(8,128)(2,1)} copy(bf16[128,128,256]{0,1,2:T(8,128)(2,1)} %fusion.4) | data formatting | bytes 16777216 | tf_op jit(solution)/shard_map/sub | solution.py:54
  192.6 14.5 %convolution_convert_fusion = bf16[16384,256]{1,0:T(8,128)(2,1)} fusion(bf16[16384,256]{1,0:T(8,128)(2,1)} %bitcast.41, bf16[16384,256]{1,0:T(8,128)(2,1)} %bitcast.40, f32[512]{0:T(512)S(1)} %get-tuple-element.12, s32[256]{0:T(256)S(1)} %iota_add_fusion, s32[512]{0:T(512)S(1)} %pad_add_fusion, f32[512]{0:T(512)S(1)} %get-tuple-element.11, ...), kind=kOutput, calls=%fused_computation | convolution fusion | flops 4335075328 | bytes 25173504 | tf_op jit(solution)/shard_map/dot_general | solution.py:95
  (26 shorter events, 0.4 us)
Async XLA Ops:
  6.5 37.6 %copy-start = (bf16[16,8,2048]{2,1,0:T(8,128)(2,1)S(1)}, bf16[16,8,2048]{2,1,0:T(8,128)(2,1)}, u32[]{:S(2)}) copy-start(bf16[16,8,2048]{2,1,0:T(8,128)(2,1)} %param.4) | copy-start | bytes 1572868
  6.5 111.8 %all-gather.3.cloned.1.call-start = ((), (), s32[]{:S(2)}) async-start(), calls=%async_computation | async-start | bytes 2228224 | tf_op jit(solution)/shard_map/all_gather | solution.py:83
  44.2 34.6 %copy-start.2 = (s32[16,8]{0,1:T(8,128)S(1)}, s32[16,8]{0,1:T(8,128)}, u32[]{:S(2)}) copy-start(s32[16,8]{0,1:T(8,128)} %param.6) | copy-start | bytes 1540
  44.2 35.5 %copy-start.3 = (s32[16,2]{0,1:T(2,128)S(1)}, s32[16,2]{0,1:T(2,128)}, u32[]{:S(2)}) copy-start(s32[16,2]{0,1:T(2,128)} %param.7) | copy-start | bytes 388
  192.6 14.5 %copy-start.1 = (bf16[16,8,2048]{2,1,0:T(8,128)(2,1)S(1)}, bf16[16,8,2048]{2,1,0:T(8,128)(2,1)}, u32[]{:S(2)}) copy-start(bf16[16,8,2048]{2,1,0:T(8,128)(2,1)} %param.4) | copy-start | bytes 1572868
Sparse Core Ops, SparseCore 0:
  79.8 38.4 all-gather.2
